TPU v7x, 32 devices: a whole 2x2x4 slice. The times are simulated.
32 devices in a mesh: grp: 2 (over y), row: 4 (over z), mic: 2 (over x), orient: 2 (over core).
Axes of the slice: x: 2, y: 2, z: 4, core: 2. Of those that a mesh axis runs over, the one named last changes fastest.
Arguments:
- spectra: bfloat16 [8, 2, 2048, 2048], P(('grp', 'mic'), None, 'row'), parts along dimension 0, may hold values from -6 to 6
- bank: bfloat16 [8, 384, 384], replicated, as said below
- orient_index: int32 [16], P('grp'), parts along dimension 0, may hold values from 0 to 7, as said below
Outputs:
- peak_map: float32 [8, 4, 512, 128], P(('grp', 'mic'), 'row'), parts along dimension 0
- power_map: float32 [8, 4, 512, 128], P(('grp', 'mic'), 'row'), parts along dimension 0
There are 2 independent parts, one for each index of `grp`. A program takes and returns all parts, laid end to end along the dimension named above; an argument that names none is the same for every part. Nothing has to cross between parts.
Inputs may be any that keep to these rules, and one draw needn't show every extreme that they name: `bank`: projection images of the table. `orient_index`: each entry names one projection of the table; entries may repeat.
All inputs are finite; a program needn't handle non-finite values.
Results may differ from a plain program's by a relative error of at most 0.0051.
Values may be sent and summed in bfloat16 or wider, within the bound.
A program may use at most 128 MiB of HBM per device.

v0:
```python
import math

import jax
import jax.numpy as jnp
from jax import lax
from jax.sharding import PartitionSpec as P

WCOLS = 128


two_pi = 2.0 * math.pi


def swapped(shard, axis, apart):
    return lax.ppermute(shard, axis, [(i, i ^ 1 << apart) for i in range(lax.axis_size(axis))])


def merged_2(part, axis, combine):
    gathered = jax.tree.map(lambda a: lax.all_gather(a, axis), part)

    def take(source):
        return jax.tree.map(lambda a: lax.dynamic_index_in_dim(a, source, 0, False), gathered)

    return lax.fori_loop(
        1, lax.axis_size(axis), lambda source, state: combine(state, take(source)), take(0)
    )


def phase_table(row_start, row_count, col_start, col_count, period):
    row_ids = row_start + jnp.arange(row_count, dtype=jnp.int32)
    col_ids = col_start + jnp.arange(col_count, dtype=jnp.int32)
    wrapped = row_ids[:, None] * col_ids[None, :] % period
    angles = wrapped.astype(jnp.float32) * (two_pi / period)
    return (jnp.cos(angles), jnp.sin(angles))


def normalize(picture):
    values = picture.astype(jnp.float32)
    centred = values - jnp.mean(values)
    factor = lax.rsqrt(jnp.mean(centred * centred) + 1e-06)
    return (centred * factor).astype(jnp.bfloat16)


def reverse_bits(number, digits):
    result = number * 0
    for digit in range(digits):
        result = result + number // (1 << digit) % 2 * (1 << digits - 1 - digit)
    return result


def combine_maps(first_pair, second_pair):
    return (jnp.maximum(first_pair[0], second_pair[0]), first_pair[1] + second_pair[1])


def shards(spectra, bank, orient_index):
    mic_count = spectra.shape[0]
    band_rows = spectra.shape[2]
    length = spectra.shape[3]
    tsize_px = bank.shape[1]
    row_devices = lax.axis_size("row")
    row_place = lax.axis_index("row")
    mic_devices = lax.axis_size("mic")
    mic_place = lax.axis_index("mic")
    share_count = orient_index.shape[0] // lax.axis_size("orient")
    chosen = lax.dynamic_slice_in_dim(
        orient_index, lax.axis_index("orient") * share_count, share_count
    )
    templates = jax.vmap(normalize)(bank[chosen])
    cos_y, sin_y = phase_table(row_place * band_rows, band_rows, 0, tsize_px, length)
    left_table = jnp.concatenate([cos_y.astype(jnp.bfloat16), -sin_y.astype(jnp.bfloat16)], 0)
    rowpass = jnp.einsum(
        "ay,oyx->oax", left_table, templates, preferred_element_type=jnp.float32
    ).astype(jnp.bfloat16)
    kx_share = length // mic_devices
    cos_x, sin_x = phase_table(0, tsize_px, mic_place * kx_share, kx_share, length)
    right_table = jnp.concatenate([cos_x.astype(jnp.bfloat16), sin_x.astype(jnp.bfloat16)], 1)
    mixed = jnp.einsum("oax,xk->oak", rowpass, right_table, preferred_element_type=jnp.float32)
    upper_rows = mixed[:, :band_rows]
    lower_rows = mixed[:, band_rows:]
    spec_re = upper_rows[:, :, :kx_share] + lower_rows[:, :, kx_share:]
    spec_im = lower_rows[:, :, :kx_share] - upper_rows[:, :, kx_share:]
    own_spectra = jnp.stack([spec_re, spec_im], 1).astype(jnp.bfloat16)
    piece = lax.all_gather(own_spectra, "mic", axis=3, tiled=True)
    width = piece.shape[3]
    cos_e, sin_e = phase_table(jnp.int32(0), width, 0, WCOLS, length)
    row_table = jnp.concatenate([cos_e.astype(jnp.bfloat16), sin_e.astype(jnp.bfloat16)], 1)
    updates = []
    for orient_pos in range(piece.shape[0]):
        tmpl_re = piece[orient_pos, 0].astype(jnp.float32)
        tmpl_im = piece[orient_pos, 1].astype(jnp.float32)
        mic_re = spectra[:, 0].astype(jnp.float32)
        mic_im = spectra[:, 1].astype(jnp.float32)
        prod_re = mic_re * tmpl_re + mic_im * tmpl_im
        prod_im = mic_im * tmpl_re - mic_re * tmpl_im
        product = jnp.stack([prod_re, prod_im], 1).astype(jnp.bfloat16)
        summed = jnp.einsum("mcbk,kw->mcbw", product, row_table, preferred_element_type=jnp.float32)
        part_re = summed[:, 0, :, :WCOLS] - summed[:, 1, :, WCOLS:]
        part_im = summed[:, 0, :, WCOLS:] + summed[:, 1, :, :WCOLS]
        updates.append(jnp.stack([part_re, part_im], 1))
    partial_value = jnp.stack(updates, 1)
    item_total = mic_count * share_count
    flat = partial_value.reshape(item_total, 2, band_rows, WCOLS)
    sections = row_devices.bit_length() - 1
    values = flat
    for bit in reversed(range(sections)):
        half_span = 1 << bit
        partner = swapped(values, "row", bit)
        upper_side = row_place // half_span % 2
        offset = row_place % half_span
        twist = offset.astype(jnp.float32) * (math.pi / half_span)
        twist_re = jnp.cos(twist)
        twist_im = jnp.sin(twist)
        differ = partner - values
        rot_re = differ[:, 0] * twist_re - differ[:, 1] * twist_im
        rot_im = differ[:, 0] * twist_im + differ[:, 1] * twist_re
        rotated = jnp.stack([rot_re, rot_im], 1)
        values = jnp.where(upper_side == 1, rotated, values + partner)
    residue = reverse_bits(row_place, sections)
    pixel_rows = residue + row_devices * jnp.arange(band_rows, dtype=jnp.int32)
    local_rows = jnp.arange(band_rows, dtype=jnp.int32)
    wrapped_col = pixel_rows[:, None] * local_rows[None, :] % length
    col_angles = wrapped_col.astype(jnp.float32) * (two_pi / length)
    column_table = jnp.stack([jnp.cos(col_angles), -jnp.sin(col_angles)], 1)
    corr = jnp.einsum("tcj,icjw->itw", column_table, values, precision=lax.Precision.HIGHEST)
    corr = corr * (1.0 / (length * tsize_px))
    corr = corr.reshape(mic_count, share_count, band_rows, WCOLS)
    peak_part = jnp.max(corr, axis=1)
    power_part = jnp.sum(corr * corr, axis=1)
    merged = merged_2((peak_part, power_part), "orient", combine_maps)
    return (merged[0][:, None], merged[1][:, None])


def solution(mesh):
    return jax.shard_map(
        shards,
        mesh=mesh,
        in_specs=(P(("grp", "mic"), None, "row", None), P(), P("grp")),
        out_specs=(P(("grp", "mic"), "row", None, None), P(("grp", "mic"), "row", None, None)),
        check_vma=False,
    )
```

profile of v0, /device:TPU:0, one launch (start us, length us, event | category | flops | bytes accessed | tf_op | source)
XLA Modules:
  0.0 665.7 jit_solution(2914393372446859276)
XLA Ops:
  7.2 3.8 cosine_convert_fusion.2
  11.0 3.8 fusion.100
  17.3 6.5 cosine_convert_fusion
  23.8 18.0 %fusion.40 = f32[4,1024,2048]{2,1,0:T(8,128)} fusion(bf16[384,1024]{1,0:T(8,128)(2,1)S(1)} %get-tuple-element.59, bf16[384,1024]{1,0:T(8,128)(2,1)S(1)} %get-tuple-element.58, bf16[4,384,384]{2,1,0:T(8,128)(2,1)S(1)} %gather_fusion, f32[4]{0:T(128)S(1)} %add_rsqrt_fusion, f32[4]{0:T(128)S(1)} %broadcast_multiply_fusion, bf16[512,384]{1,0:T(8,128)(2,1)} %fusion.100, ...), kind=kOutput, calls=%fused_computation.63 | convolution fusion | flops 7659061248 | bytes 37093408 | tf_op jit(solution)/shard_map/oax,xk->oak/dot_general | solution.py:77
  41.8 14.6 %fusion.34 = (bf16[4,1,512,1024]{3,2,0,1:T(8,128)(2,1)S(1)}, bf16[4,1,512,1024]{3,2,0,1:T(8,128)(2,1)}) fusion(f32[4,1024,2048]{2,1,0:T(8,128)} %fusion.40), kind=kLoop, calls=%fused_computation.54 | loop fusion | flops 8388608 | bytes 41943040 | tf_op jit(solution)/shard_map/stack | solution.py:82
  56.3 6.2 pad_maximum_fusion
  62.6 5.0 sine_convert_fusion.1
  67.6 196.7 %all-gather.6.cloned.1.call-done = bf16[4,2,512,2048]{3,2,0,1:T(8,128)(2,1)} async-done(((bf16[4,2,512,1024]{3,2,0,1:T(8,128)(2,1)}), bf16[4,2,512,2048]{3,2,0,1:T(8,128)(2,1)}) %all-gather.6.cloned.1.call-update) | async-done | bytes 16777232 | tf_op jit(solution)/shard_map/all_gather | solution.py:83
  264.3 14.2 %fusion.56 = (f32[512,2048]{1,0:T(8,128)S(1)}, f32[512,2048]{1,0:T(8,128)}, f32[512,2048]{1,0:T(8,128)}, f32[512,2048]{1,0:T(8,128)}, f32[512,2048]{1,0:T(8,128)...) fusion(bf16[4,2,512,2048]{3,2,0,1:T(8,128)(2,1)} %all-gather.6.cloned.1.call-done), kind=kLoop, calls=%fused_computation.91 | loop fusion | flops 8388608 | bytes 50331648 | tf_op jit(solution)/shard_map/convert_element_type | solution.py:89
  278.5 19.2 %fusion.1 = (bf16[2,1,512,2048]{3,2,1,0:T(8,128)(2,1)}, bf16[2,1,512,2048]{3,2,1,0:T(8,128)(2,1)}, bf16[2,1,512,2048]{3,2,1,0:T(8,128)(2,1)}, bf16[2,1,512,2048]...) fusion(f32[512,2048]{1,0:T(8,128)} %get-tuple-element.35, ...), kind=kLoop, calls=%fused_computation.18 | loop fusion | flops 54525952 | bytes 58720256 | tf_op jit(solution)/shard_map/convert.14
  297.8 5.2 fusion.18
  306.4 5.2 fusion.5
  311.6 5.2 fusion.22
  321.0 2.4 fusion.30
  326.4 2.4 collective-permute-start
  329.0 180.8 %collective-permute-done = f32[8,2,512,128]{3,2,1,0:T(8,128)} collective-permute-done((f32[8,2,512,128]{3,2,1,0:T(8,128)}, f32[8,2,512,128]{3,2,1,0:T(8,128)}, u32[]{:S(2)}, u32[]{:S(2)}) %collective-permute-start) | collective-permute-done | bytes 4194336 | tf_op jit(solution)/shard_map/ppermute | solution.py:15
  509.8 3.9 bitcast_subtract_fusion
  514.2 6.2 maximum_select_fusion
  520.9 4.2 fusion.99
  525.1 87.2 %collective-permute-done.1 = f32[8,2,512,128]{3,2,1,0:T(8,128)} collective-permute-done((f32[8,2,512,128]{3,2,1,0:T(8,128)}, f32[8,2,512,128]{3,2,1,0:T(8,128)}, u32[]{:S(2)}, u32[]{:S(2)}) %collective-permute-start.1) | collective-permute-done | bytes 4194336 | tf_op jit(solution)/shard_map/ppermute | solution.py:15
  612.3 4.1 sub.78
  616.8 16.4 %fusion.59 = (f32[2,512,128]{1,2,0:T(8,128)S(1)}, f32[2,512,128]{1,2,0:T(8,128)S(1)}) fusion(f32[512,1,512]{2,0,1:T(8,128)S(1)} %get-tuple-element.61, f32[512,1,512]{2,0,1:T(8,128)S(1)} %get-tuple-element.60, f32[8,1,512,128]{3,2,1,0:T(8,128)S(1)} %get-tuple-element.47, f32[8,1,512,128]{3,2,1,0:T(8,128)S(1)} %get-tuple-element.46, ...), kind=kOutput, calls=%fused_computation.97 | convolution fusion | flops 6447955968 | bytes 15728641 | tf_op jit(solution)/shard_map/tcj,icjw->itw/dot_general | solution.py:124
  635.3 9.1 %all-gather.10.cloned.1.call-done = f32[4,512,128]{2,1,0:T(8,128)} async-done(((f32[2,512,128]{2,1,0:T(8,128)}), f32[4,512,128]{2,1,0:T(8,128)}) %all-gather.10.cloned.1.call-update) | async-done | bytes 1048592 | tf_op jit(solution)/shard_map/all_gather | solution.py:19
  646.4 10.3 %all-gather.8.cloned.1.call-done = f32[4,512,128]{2,1,0:T(8,128)} async-done(((f32[2,512,128]{2,1,0:T(8,128)}), f32[4,512,128]{2,1,0:T(8,128)}) %all-gather.8.cloned.1.call-update) | async-done | bytes 1048592 | tf_op jit(solution)/shard_map/all_gather | solution.py:19
  (59 shorter events, 20.5 us)
Async XLA Ops:
  7.2 8.5 %copy-start = (bf16[8,384,384]{2,1,0:T(8,128)(2,1)S(1)}, bf16[8,384,384]{2,1,0:T(8,128)(2,1)}, u32[]{:S(2)}) copy-start(bf16[8,384,384]{2,1,0:T(8,128)(2,1)} %param.4) | copy-start | bytes 7077892
  7.2 257.1 %all-gather.6.cloned.1.call-start = ((), (), s32[]{:S(2)}) async-start(), calls=%async_computation | async-start | bytes 25165824 | tf_op jit(solution)/shard_map/all_gather | solution.py:83
  62.6 581.7 %all-gather.10.cloned.1.call-start = ((), (), s32[]{:S(2)}) async-start(), calls=%async_computation.2 | async-start | bytes 1572864 | tf_op jit(solution)/shard_map/all_gather | solution.py:19
  297.7 5.4 slice-start
  297.7 6.2 slice-start.1
  297.8 7.4 %copy-start.2 = (f32[512,2048]{1,0:T(8,128)S(1)}, f32[512,2048]{1,0:T(8,128)}, u32[]{:S(2)}) copy-start(f32[512,2048]{1,0:T(8,128)} %get-tuple-element.33) | copy-start | bytes 12582916
  297.8 8.6 %copy-start.3 = (f32[512,2048]{1,0:T(8,128)S(1)}, f32[512,2048]{1,0:T(8,128)}, u32[]{:S(2)}) copy-start(f32[512,2048]{1,0:T(8,128)} %get-tuple-element.34) | copy-start | bytes 12582916
  306.4 5.2 copy-start.8
  306.4 5.2 copy-start.9
  311.6 5.3 copy-start.6
  311.6 5.9 copy-start.7
  317.5 2.5 copy-start.4
  317.5 3.5 copy-start.5
  326.4 183.4 %collective-permute-start = (f32[8,2,512,128]{3,2,1,0:T(8,128)}, f32[8,2,512,128]{3,2,1,0:T(8,128)}, u32[]{:S(2)}, u32[]{:S(2)}) collective-permute-start(f32[8,2,512,128]{3,2,1,0:T(8,128)} %bitcast.20), channel_id=1, source_target_pairs={{0,8},{4,12},{8,0},{12,4},{1,9},{5,13},{9,1},{13,5},{2,10},{6,14},... | collective-permute-start | bytes 12582920 | tf_op jit(solution)/shard_map/ppermute | solution.py:15
  520.4 91.9 %collective-permute-start.1 = (f32[8,2,512,128]{3,2,1,0:T(8,128)}, f32[8,2,512,128]{3,2,1,0:T(8,128)}, u32[]{:S(2)}, u32[]{:S(2)}) collective-permute-start(f32[8,2,512,128]{3,2,1,0:T(8,128)} %maximum_select_fusion), channel_id=1, source_target_pairs={{0,4},{4,0},{8,12},{12,8},{1,5},{5,1},{9,13},{13,9},{2,6},{6,2},{1... | collective-permute-start | bytes 12582920 | tf_op jit(solution)/shard_map/ppermute | solution.py:15
  616.8 41.9 %copy-start.1 = (bf16[8,384,384]{2,1,0:T(8,128)(2,1)S(1)}, bf16[8,384,384]{2,1,0:T(8,128)(2,1)}, u32[]{:S(2)}) copy-start(bf16[8,384,384]{2,1,0:T(8,128)(2,1)} %param.4) | copy-start | bytes 7077892
  634.2 22.5 %all-gather.8.cloned.1.call-start = ((), (), s32[]{:S(2)}) async-start(), calls=%async_computation.1 | async-start | bytes 1572864 | tf_op jit(solution)/shard_map/all_gather | solution.py:19
Sparse Core Ops, SparseCore 0:
  62.7 201.5 all-gather.5
  634.3 9.9 all-gather.9
  646.4 10.1 all-gather.7
where the time goes:
time: 674 us; the launch traced here: 666 us
  waiting for transfers between devices  484 us (72%)
  other arithmetic  104 us (15%)
  matrix products  49.5 us (7%)
  between operations  14.6 us (2%)
  local copies, waits for them, and re-layouts  9.96 us (1%)
    ppermute x2, waiting for transfers between devices, swapped(): lax.ppermute(shard, axis, [(i, i ^ 1 << apart) for i in range(lax.axis_si...  268 us
    all_gather x1, waiting for transfers between devices, shards(): piece = lax.all_gather(own_spectra, 'mic', axis=3, tiled=True)  197 us
    another operation x2, other arithmetic  24.4 us
    another operation x2, other arithmetic, shards(): own_spectra = jnp.stack([spec_re, spec_im], 1).astype(jnp.bfloat16)  20.8 us
    all_gather x2, waiting for transfers between devices, merged_2(): gathered = jax.tree.map(lambda a: lax.all_gather(a, axis), part)  19.4 us
    dot_general x1, matrix products, shards(): jnp.einsum('oax,xk->oak', rowpass, right_table, preferred_element_type=jn...  18 us
    dot_general x1, matrix products, shards(): jnp.einsum('tcj,icjw->itw', column_table, values, precision=lax.Precision...  16.4 us
    dot_general x4, matrix products, shards(): jnp.einsum('mcbk,kw->mcbw', product, row_table, preferred_element_type=jn...  15.2 us
  transfers between devices with their start and end apart: 5, of which 5 were waited for; matrix products, arithmetic and copies ran while one was open for 2% of the time, Pallas kernels for 0%

commit v1 on v0

--- a/solution.py
+++ b/solution.py
@@ -1,11 +1,17 @@
+import functools
 import math
 
 import jax
 import jax.numpy as jnp
+import numpy as np
 from jax import lax
+from jax.experimental import pallas as pl
+from jax.experimental.pallas import tpu as pltpu
 from jax.sharding import PartitionSpec as P
 
 WCOLS = 128
+MESH = pl.DeviceIdType.MESH
+BLK = 16
 
 
 two_pi = 2.0 * math.pi
@@ -52,15 +58,13 @@
     return (jnp.maximum(first_pair[0], second_pair[0]), first_pair[1] + second_pair[1])
 
 
-def shards(spectra, bank, orient_index):
+def shards_general(spectra, bank, orient_index):
     mic_count = spectra.shape[0]
     band_rows = spectra.shape[2]
     length = spectra.shape[3]
     tsize_px = bank.shape[1]
     row_devices = lax.axis_size("row")
     row_place = lax.axis_index("row")
-    mic_devices = lax.axis_size("mic")
-    mic_place = lax.axis_index("mic")
     share_count = orient_index.shape[0] // lax.axis_size("orient")
     chosen = lax.dynamic_slice_in_dim(
         orient_index, lax.axis_index("orient") * share_count, share_count
@@ -71,21 +75,18 @@
     rowpass = jnp.einsum(
         "ay,oyx->oax", left_table, templates, preferred_element_type=jnp.float32
     ).astype(jnp.bfloat16)
-    kx_share = length // mic_devices
-    cos_x, sin_x = phase_table(0, tsize_px, mic_place * kx_share, kx_share, length)
+    cos_x, sin_x = phase_table(0, tsize_px, 0, length, length)
     right_table = jnp.concatenate([cos_x.astype(jnp.bfloat16), sin_x.astype(jnp.bfloat16)], 1)
     mixed = jnp.einsum("oax,xk->oak", rowpass, right_table, preferred_element_type=jnp.float32)
     upper_rows = mixed[:, :band_rows]
     lower_rows = mixed[:, band_rows:]
-    spec_re = upper_rows[:, :, :kx_share] + lower_rows[:, :, kx_share:]
-    spec_im = lower_rows[:, :, :kx_share] - upper_rows[:, :, kx_share:]
-    own_spectra = jnp.stack([spec_re, spec_im], 1).astype(jnp.bfloat16)
-    piece = lax.all_gather(own_spectra, "mic", axis=3, tiled=True)
-    width = piece.shape[3]
-    cos_e, sin_e = phase_table(jnp.int32(0), width, 0, WCOLS, length)
+    spec_re = upper_rows[:, :, :length] + lower_rows[:, :, length:]
+    spec_im = lower_rows[:, :, :length] - upper_rows[:, :, length:]
+    piece = jnp.stack([spec_re, spec_im], 1).astype(jnp.bfloat16)
+    cos_e, sin_e = phase_table(0, length, 0, WCOLS, length)
     row_table = jnp.concatenate([cos_e.astype(jnp.bfloat16), sin_e.astype(jnp.bfloat16)], 1)
     updates = []
-    for orient_pos in range(piece.shape[0]):
+    for orient_pos in range(share_count):
         tmpl_re = piece[orient_pos, 0].astype(jnp.float32)
         tmpl_im = piece[orient_pos, 1].astype(jnp.float32)
         mic_re = spectra[:, 0].astype(jnp.float32)
@@ -99,9 +100,8 @@
         updates.append(jnp.stack([part_re, part_im], 1))
     partial_value = jnp.stack(updates, 1)
     item_total = mic_count * share_count
-    flat = partial_value.reshape(item_total, 2, band_rows, WCOLS)
+    values = partial_value.reshape(item_total, 2, band_rows, WCOLS)
     sections = row_devices.bit_length() - 1
-    values = flat
     for bit in reversed(range(sections)):
         half_span = 1 << bit
         partner = swapped(values, "row", bit)
@@ -130,6 +130,376 @@
     return (merged[0][:, None], merged[1][:, None])
 
 
+def factors(rows, cols, period, shift=None):
+    angle = np.outer(rows, cols) % period * (two_pi / period)
+    if shift is not None:
+        angle = angle + shift
+    return np.stack([np.cos(angle), np.sin(angle)]).astype(np.float32)
+
+
+def fused_kernel(
+    sizes,
+    index_ref, spectra_ref, bank_ref,
+    left_a, left_b, tx_a, tx_b, te_a, te_b, col_a, col_b, tw_a, tw_b,
+    peak_ref, power_ref,
+    spec, left, table_x, table_e, col_hi, col_lo, twc, tws,
+    rows_in, acc, send, recv, v_hi, v_lo, peak, power,
+    own, sibling, merged, final,
+    spec_sem, send_sem, recv_sem, pair_send, pair_recv,
+    map_send, map_recv, fwd_send, fwd_recv,
+):
+    bands, share, band, length, tsize = sizes
+    half = WCOLS // 2
+    me = lax.axis_index("row")
+    core = lax.axis_index("orient")
+
+    barrier = pltpu.get_barrier_semaphore()
+    for k in range(1, bands):
+        pl.semaphore_signal(
+            barrier, inc=1, device_id={"row": lax.rem(me + k, bands)}, device_id_type=MESH
+        )
+    pl.semaphore_signal(barrier, inc=1, device_id={"orient": 1 - core}, device_id_type=MESH)
+
+    load = pltpu.make_async_copy(spectra_ref, spec, spec_sem)
+    load.start()
+
+    def rows_of(block):
+        return pl.ds(pl.multiple_of(block * BLK, BLK), BLK)
+
+    def left_body(a, carry):
+        row = me * (band // BLK) + a
+        ca, sa = left_a[0, pl.ds(row, 1), :], left_a[1, pl.ds(row, 1), :]
+        cb, sb = left_b[0], left_b[1]
+        left[0, rows_of(a), :] = (ca * cb - sa * sb).astype(jnp.bfloat16)
+        left[1, rows_of(a), :] = (-(sa * cb + ca * sb)).astype(jnp.bfloat16)
+        return carry
+
+    lax.fori_loop(0, band // BLK, left_body, 0)
+
+    def tx_body(a, carry):
+        ca, sa = tx_a[0, pl.ds(a, 1), :], tx_a[1, pl.ds(a, 1), :]
+        cb, sb = tx_b[0], tx_b[1]
+        table_x[rows_of(a), :] = (ca * cb - sa * sb).astype(jnp.bfloat16)
+        table_x[rows_of(a + tsize // BLK), :] = (sa * cb + ca * sb).astype(jnp.bfloat16)
+        return carry
+
+    lax.fori_loop(0, tsize // BLK, tx_body, 0)
+
+    def te_body(a, carry):
+        ca, sa = te_a[0, pl.ds(a, 1), :], te_a[1, pl.ds(a, 1), :]
+        for part in range(2):
+            cb, sb = te_b[part, 0], te_b[part, 1]
+            table_e[part, rows_of(a), :] = (ca * cb - sa * sb).astype(jnp.bfloat16)
+        return carry
+
+    lax.fori_loop(0, length // BLK, te_body, 0)
+
+    def col_body(a, carry):
+        ca, sa = col_a[0, pl.ds(a, 1), :], col_a[1, pl.ds(a, 1), :]
+        value = ca * col_b[0] - sa * col_b[1]
+        high = value.astype(jnp.bfloat16)
+        col_hi[rows_of(a), :] = high
+        col_lo[rows_of(a), :] = (value - high.astype(jnp.float32)).astype(jnp.bfloat16)
+        ta, ua = tw_a[0, pl.ds(a, 1), :], tw_a[1, pl.ds(a, 1), :]
+        tb, ub = tw_b[0], tw_b[1]
+        lane = lax.broadcasted_iota(jnp.int32, (BLK, 3 * WCOLS), 1) % WCOLS
+        twc[rows_of(a), :] = ta * tb - ua * ub
+        sine = ua * tb + ta * ub
+        tws[rows_of(a), :] = jnp.where(lane < half, -sine, sine)
+        return carry
+
+    lax.fori_loop(0, band // BLK, col_body, 0)
+
+    pl.semaphore_wait(barrier, bands)
+    load.wait()
+
+    kt = 256
+
+    def orient_body(o, carry):
+        picture = bank_ref[index_ref[core * share + o]].astype(jnp.float32)
+        centred = picture - jnp.mean(picture)
+        scale = lax.rsqrt(jnp.mean(centred * centred) + 1e-06)
+        template = (centred * scale).astype(jnp.bfloat16)
+        pass_re = jnp.dot(left[0], template, preferred_element_type=jnp.float32)
+        pass_im = jnp.dot(left[1], template, preferred_element_type=jnp.float32)
+        pass_re = pass_re.astype(jnp.bfloat16)
+        pass_im = pass_im.astype(jnp.bfloat16)
+        rows_in[0, :, pl.ds(0, tsize)] = pass_re
+        rows_in[0, :, pl.ds(tsize, tsize)] = pass_im
+        rows_in[1, :, pl.ds(0, tsize)] = pass_im
+        rows_in[1, :, pl.ds(tsize, tsize)] = -pass_re
+        acc[...] = jnp.zeros_like(acc)
+
+        def kx_body(k, inner):
+            cols = pl.ds(pl.multiple_of(k * kt, kt), kt)
+            wide = table_x[:, cols]
+            t_re = jnp.dot(rows_in[0], wide, preferred_element_type=jnp.float32)
+            t_im = jnp.dot(rows_in[1], wide, preferred_element_type=jnp.float32)
+            t_re = t_re.astype(jnp.bfloat16).astype(jnp.float32)
+            t_im = t_im.astype(jnp.bfloat16).astype(jnp.float32)
+            for m in range(2):
+                m_re = spec[m, 0, :, cols].astype(jnp.float32)
+                m_im = spec[m, 1, :, cols].astype(jnp.float32)
+                p_re = (m_re * t_re + m_im * t_im).astype(jnp.bfloat16)
+                p_im = (m_im * t_re - m_re * t_im).astype(jnp.bfloat16)
+                acc[m] += jnp.dot(
+                    p_re, table_e[0, cols, :], preferred_element_type=jnp.float32
+                ) + jnp.dot(p_im, table_e[1, cols, :], preferred_element_type=jnp.float32)
+            return inner
+
+        lax.fori_loop(0, length // kt, kx_body, 0)
+        for d in range(bands):
+            tile = acc[d // 2, :, pl.ds(d % 2 * WCOLS, WCOLS)].astype(jnp.bfloat16)
+
+            @pl.when(me == d)
+            def _():
+                recv[me, o] = tile
+
+            @pl.when(me != d)
+            def _():
+                send[d, o] = tile
+
+        for k in (2, 1, 3):
+            dest = lax.rem(me + k, bands)
+            pltpu.make_async_remote_copy(
+                src_ref=send.at[dest, o], dst_ref=recv.at[me, o],
+                send_sem=send_sem.at[k, o], recv_sem=recv_sem.at[me, o],
+                device_id={"row": dest}, device_id_type=MESH,
+            ).start()
+        return carry
+
+    lax.fori_loop(0, share, orient_body, 0)
+
+    peak[...] = jnp.full_like(peak, -1e30)
+    power[...] = jnp.zeros_like(power)
+    factor = 1.0 / (length * tsize)
+    rc = 64
+
+    def column_body(o, carry):
+        for k in range(1, bands):
+            source = lax.rem(me + k, bands)
+            pltpu.make_async_remote_copy(
+                src_ref=send.at[source, o], dst_ref=recv.at[source, o],
+                send_sem=send_sem.at[k, o], recv_sem=recv_sem.at[source, o],
+                device_id={"row": source}, device_id_type=MESH,
+            ).wait_recv()
+
+        def chunk(c, inner):
+            rows = pl.ds(pl.multiple_of(c * rc, rc), rc)
+            lane = lax.broadcasted_iota(jnp.int32, (rc, WCOLS), 1)
+            first = lane < half
+            b0, b1, b2, b3 = [recv[b, o, rows, :].astype(jnp.float32) for b in range(4)]
+            s02, d02, s13, d13 = b0 + b2, b0 - b2, b1 + b3, b1 - b3
+            turned = pltpu.roll(d13, half, 1)
+            turned = jnp.where(first, -turned, turned)
+            u = [s02 + s13, d02 + turned, s02 - s13, d02 - turned]
+            v = [u[0]]
+            for rho in range(1, 4):
+                span = pl.ds((rho - 1) * WCOLS, WCOLS)
+                v.append(u[rho] * twc[rows, span] + pltpu.roll(u[rho], half, 1) * tws[rows, span])
+            for pair in range(2):
+                even, odd = v[2 * pair], v[2 * pair + 1]
+                v_re = jnp.where(first, even, pltpu.roll(odd, half, 1))
+                v_im = jnp.where(first, pltpu.roll(even, half, 1), odd)
+                span = pl.ds(pair * WCOLS, WCOLS)
+                for part, value in enumerate((v_re, v_im)):
+                    high = value.astype(jnp.bfloat16)
+                    where = pl.ds(pl.multiple_of(part * band + c * rc, rc), rc)
+                    v_hi[where, span] = high
+                    v_lo[where, span] = (value - high.astype(jnp.float32)).astype(jnp.bfloat16)
+            return inner
+
+        lax.fori_loop(0, band // rc, chunk, 0)
+        corr = jnp.dot(col_hi[...], v_hi[...], preferred_element_type=jnp.float32)
+        corr += jnp.dot(col_lo[...], v_hi[...], preferred_element_type=jnp.float32)
+        corr += jnp.dot(col_hi[...], v_lo[...], preferred_element_type=jnp.float32)
+        corr = corr * factor
+        peak[...] = jnp.maximum(peak[...], corr)
+        power[...] += corr * corr
+        return carry
+
+    lax.fori_loop(0, share, column_body, 0)
+
+    first = lax.broadcasted_iota(jnp.int32, (band, WCOLS), 1) < half
+    for q in range(4):
+        rho = (q % 2) * 2 + q // 2
+        span = pl.ds(rho // 2 * WCOLS, WCOLS)
+        hi, po = peak[:, span], power[:, span]
+        if rho % 2 == 0:
+            own[q] = jnp.where(first, hi, pltpu.roll(po, half, 1))
+        else:
+            own[q] = jnp.where(first, pltpu.roll(hi, half, 1), po)
+
+    hb = band // 2
+    mine = pl.ds(pl.multiple_of(core * hb, hb), hb)
+    theirs = pl.ds(pl.multiple_of((1 - core) * hb, hb), hb)
+    swap = pltpu.make_async_remote_copy(
+        src_ref=own.at[:, theirs, :], dst_ref=sibling,
+        send_sem=pair_send, recv_sem=pair_recv,
+        device_id={"orient": 1 - core}, device_id_type=MESH,
+    )
+    swap.start()
+    swap.wait()
+    first = lax.broadcasted_iota(jnp.int32, (hb, WCOLS), 1) < half
+    for q in range(4):
+        one, two = own[q, mine, :], sibling[q]
+        total = jnp.where(first, jnp.maximum(one, two), one + two)
+
+        @pl.when(me == q)
+        def _():
+            final[me, mine, :] = total
+
+        @pl.when(me != q)
+        def _():
+            merged[q] = total
+
+    def map_copy(k, source):
+        dest = lax.rem(me + k, bands)
+        return pltpu.make_async_remote_copy(
+            src_ref=merged.at[dest], dst_ref=final.at[source, mine, :],
+            send_sem=map_send.at[k], recv_sem=map_recv.at[source],
+            device_id={"row": dest}, device_id_type=MESH,
+        )
+
+    def forward(source, rows):
+        return pltpu.make_async_remote_copy(
+            src_ref=final.at[source, rows, :], dst_ref=final.at[source, rows, :],
+            send_sem=fwd_send.at[source], recv_sem=fwd_recv.at[source],
+            device_id={"orient": 1 - core}, device_id_type=MESH,
+        )
+
+    for k in (2, 1, 3):
+        map_copy(k, me).start()
+    forward(me, mine).start()
+    for k in (1, 3, 2):
+        source = lax.rem(me + k, bands)
+        map_copy(k, source).wait_recv()
+        forward(source, mine).start()
+    for source in range(4):
+        forward(source, theirs).wait_recv()
+    first = lax.broadcasted_iota(jnp.int32, (band, WCOLS), 1) < half
+    for m in range(2):
+        a, b = final[2 * m], final[2 * m + 1]
+        peak_ref[m, 0] = jnp.where(first, a, pltpu.roll(b, half, 1))
+        power_ref[m, 0] = jnp.where(first, pltpu.roll(a, half, 1), b)
+
+    for source in range(4):
+        forward(source, mine).wait_send()
+    for k in range(1, bands):
+        map_copy(k, me).wait_send()
+
+    def drain(o, carry):
+        for k in range(1, bands):
+            dest = lax.rem(me + k, bands)
+            pltpu.make_async_remote_copy(
+                src_ref=send.at[dest, o], dst_ref=recv.at[me, o],
+                send_sem=send_sem.at[k, o], recv_sem=recv_sem.at[me, o],
+                device_id={"row": dest}, device_id_type=MESH,
+            ).wait_send()
+        return carry
+
+    lax.fori_loop(0, share, drain, 0)
+
+
+def shards_fused(spectra, bank, orient_index):
+    band = spectra.shape[2]
+    length = spectra.shape[3]
+    tsize = bank.shape[1]
+    bands = lax.axis_size("row")
+    share = orient_index.shape[0] // lax.axis_size("orient")
+    half = WCOLS // 2
+    bf, f32 = jnp.bfloat16, jnp.float32
+
+    small = np.arange(BLK)
+    y = np.arange(tsize)
+    kx = np.arange(length)
+    lane = np.arange(2 * WCOLS)
+    lane_x = lane // WCOLS * half + lane % half
+    is_im = lane % WCOLS >= half
+    quarter = two_pi / 4
+    te_b = np.stack(
+        [
+            factors(small, lane_x, length, np.where(is_im, -quarter, 0.0)),
+            factors(small, lane_x, length, np.where(is_im, 0.0, quarter)),
+        ]
+    )
+    j = np.arange(band)
+    col_j = np.concatenate([j, j])
+    col_shift = np.where(np.arange(2 * band) < band, 0.0, quarter)
+    rho = np.repeat(np.arange(1, 4), WCOLS)
+    tables = [
+        factors(np.arange(length // BLK) * BLK, y, length),
+        factors(small, y, length),
+        factors(np.arange(tsize // BLK) * BLK, kx, length),
+        factors(small, kx, length),
+        factors(np.arange(length // BLK) * BLK, lane_x, length),
+        te_b,
+        factors(np.arange(band // BLK) * BLK, col_j, band),
+        factors(small, col_j, band, col_shift),
+        factors(np.arange(band // BLK) * BLK, rho, length),
+        factors(small, rho, length),
+    ]
+    out = jax.ShapeDtypeStruct((2, 1, band, WCOLS), f32)
+    vmem = pl.BlockSpec(memory_space=pltpu.VMEM)
+    dma = pltpu.SemaphoreType.DMA
+    return pl.pallas_call(
+        functools.partial(fused_kernel, (bands, share, band, length, tsize)),
+        out_shape=(out, out),
+        in_specs=[
+            pl.BlockSpec(memory_space=pltpu.SMEM),
+            pl.BlockSpec(memory_space=pl.ANY),
+        ]
+        + [vmem] * (1 + len(tables)),
+        out_specs=(vmem, vmem),
+        scratch_shapes=[
+            pltpu.VMEM((2, 2, band, length), bf),
+            pltpu.VMEM((2, band, tsize), bf),
+            pltpu.VMEM((2 * tsize, length), bf),
+            pltpu.VMEM((2, length, 2 * WCOLS), bf),
+            pltpu.VMEM((band, 2 * band), bf),
+            pltpu.VMEM((band, 2 * band), bf),
+            pltpu.VMEM((band, 3 * WCOLS), f32),
+            pltpu.VMEM((band, 3 * WCOLS), f32),
+            pltpu.VMEM((2, band, 2 * tsize), bf),
+            pltpu.VMEM((2, band, 2 * WCOLS), f32),
+            pltpu.VMEM((bands, share, band, WCOLS), bf),
+            pltpu.VMEM((bands, share, band, WCOLS), bf),
+            pltpu.VMEM((2 * band, 2 * WCOLS), bf),
+            pltpu.VMEM((2 * band, 2 * WCOLS), bf),
+            pltpu.VMEM((band, 2 * WCOLS), f32),
+            pltpu.VMEM((band, 2 * WCOLS), f32),
+            pltpu.VMEM((4, band, WCOLS), f32),
+            pltpu.VMEM((4, band // 2, WCOLS), f32),
+            pltpu.VMEM((4, band // 2, WCOLS), f32),
+            pltpu.VMEM((4, band, WCOLS), f32),
+            dma,
+            dma((bands, share)),
+            dma((bands, share)),
+            dma,
+            dma,
+            dma((bands,)),
+            dma((bands,)),
+            dma((bands,)),
+            dma((bands,)),
+        ],
+        compiler_params=pltpu.CompilerParams(
+            collective_id=0, has_side_effects=True, vmem_limit_bytes=60 << 20
+        ),
+    )(orient_index, spectra, bank, *tables)
+
+
+def shards(spectra, bank, orient_index):
+    fits = (
+        lax.axis_size("row") == 4
+        and lax.axis_size("orient") == 2
+        and spectra.shape[0] == 2
+        and spectra.shape[2] % 128 == 0
+        and spectra.shape[3] == 4 * spectra.shape[2]
+    )
+    body = shards_fused if fits else shards_general
+    return body(spectra, bank, orient_index)
+
+
 def solution(mesh):
     return jax.shard_map(
         shards,

time: 674 us -> 87.6 us (0.13); the launches traced: 666 us -> 87.3 us
  waiting for transfers between devices: 484 us -> 0 us
  other arithmetic: 104 us -> 0 us
  Pallas kernels: 0 us -> 82.9 us
  matrix products: 49.5 us -> 0 us
  between operations: 14.6 us -> 0.64 us
    ppermute x2 -> x0, waiting for transfers between devices: 268 us -> none  [swapped(): lax.ppermute(shard, axis, [(i, i ^ 1 << apart) for i in range(lax.axis_si...]
    all_gather x3 -> x0, waiting for transfers between devices: 216 us -> none  [the longest x1 197 us: shards(): piece = lax.all_gather(own_spectra, 'mic', axis=3, tiled=True)]
    pallas_call x0 -> x1, Pallas kernels: none -> 82.9 us  [shards_fused(): pl.pallas_call(functools.partial(fused_kernel, (bands, share, band, lengt...]
    dot_general x6 -> x0, matrix products: 49.5 us -> none  [the longest x1 18 us: shards(): jnp.einsum('oax,xk->oak', rowpass, right_table, preferred_element_type=jn...]
    another operation x9 -> x0, other arithmetic: 45.8 us -> none
    convert_element_type x4 -> x0, other arithmetic: 29.4 us -> none  [the longest x1 14.2 us: shards(): tmpl_re = piece[orient_pos, 0].astype(jnp.float32)]
    sub x8 -> x0, other arithmetic: 9.3 us -> none  [the longest x2 8.04 us: shards(): differ = partner - values]
    select_n x2 -> x0, other arithmetic: 6.92 us -> none  [the longest x1 6.19 us: shards(): values = jnp.where(upper_side == 1, rotated, values + partner)]
  transfers between devices with their start and end apart: 5 -> 0, of which waited for: 5 -> 0; matrix products, arithmetic and copies ran while one was open for 2% -> 0% of each run, Pallas kernels for 0% -> 0%
where the time goes in v1:
time: 87.6 us; the launch traced here: 87.3 us
  Pallas kernels  82.9 us (95%)
  local copies, waits for them, and re-layouts  3.74 us (4%)
    pallas_call x1, Pallas kernels, shards_fused(): pl.pallas_call(functools.partial(fused_kernel, (bands, share, band, lengt...  82.9 us
    unnamed x2, local copies, waits for them, and re-layouts  3.74 us

profile of v1, /device:TPU:0, one launch (start us, length us, event | category | flops | bytes accessed | tf_op | source)
XLA Modules:
  0.0 87.3 jit_solution(6261302115932632026)
XLA Ops:
  0.6 82.9 %shard_map.140 = (f32[2,1,512,128]{3,2,1,0:T(8,128)}, f32[2,1,512,128]{3,2,1,0:T(8,128)}) custom-call(s32[8]{0:T(128)} %index_ref.1, bf16[2,2,512,2048]{3,2,1,0:T(8,128)(2,1)} %spectra_ref.1, bf16[8,384,384]{2,1,0:T(8,128)(2,1)} %bank_ref.1, f32[2,128,384]{2,1,0:T(8,128)} %constant.20.clone.left_a, f32[2,16,384]{2,1,0:T(8,128)} %constant.21.clone.left_b, ...), custom_call_target="tpu_custom_call" | custom-call | tf_op jit(solution)/shard_map/pallas_call | solution.py:445
  83.5 1.9 %copy.17 = f32[2,1,512,128]{3,2,1,0:T(8,128)} copy(f32[2,1,512,128]{3,2,1,0:T(8,128)} %get-tuple-element.4) | data formatting | bytes 1048576
  85.4 1.9 %copy.18 = f32[2,1,512,128]{3,2,1,0:T(8,128)} copy(f32[2,1,512,128]{3,2,1,0:T(8,128)} %get-tuple-element.5) | data formatting | bytes 1048576

commit v2 on v1

--- a/solution.py
+++ b/solution.py
@@ -12,6 +12,8 @@
 WCOLS = 128
 MESH = pl.DeviceIdType.MESH
 BLK = 16
+PRODUCT = jnp.float32
+MAPS = jnp.bfloat16
 
 
 two_pi = 2.0 * math.pi
@@ -139,20 +141,30 @@
 
 def fused_kernel(
     sizes,
-    index_ref, spectra_ref, bank_ref,
-    left_a, left_b, tx_a, tx_b, te_a, te_b, col_a, col_b, tw_a, tw_b,
-    peak_ref, power_ref,
-    spec, left, table_x, table_e, col_hi, col_lo, twc, tws,
-    rows_in, acc, send, recv, v_hi, v_lo, peak, power,
-    own, sibling, merged, final,
-    spec_sem, send_sem, recv_sem, pair_send, pair_recv,
+    index_ref, spectra_ref, bank_ref, w384, w512, w256, w1024,
+    final,
+    spec, bank, f384, f512, f256, f1024,
+    left, table_x, table_e, col_hi, col_lo, twc, tws, order,
+    rows_in, prod, send, recv, v_hi, v_lo, peak, power,
+    own, sibling, merged,
+    load_sem, send_sem, recv_sem, pair_send, pair_recv,
     map_send, map_recv, fwd_send, fwd_recv,
 ):
     bands, share, band, length, tsize = sizes
     half = WCOLS // 2
+    hb = band // 2
+    kq = length // 4
     me = lax.axis_index("row")
     core = lax.axis_index("orient")
 
+    loads = [
+        pltpu.make_async_copy(source, target, load_sem.at[n])
+        for n, (source, target) in enumerate(
+            [(w384, f384), (w512, f512), (w256, f256), (w1024, f1024), (bank_ref, bank), (spectra_ref, spec)]
+        )
+    ]
+    for load in loads:
+        load.start()
     barrier = pltpu.get_barrier_semaphore()
     for k in range(1, bands):
         pl.semaphore_signal(
@@ -160,48 +172,151 @@
         )
     pl.semaphore_signal(barrier, inc=1, device_id={"orient": 1 - core}, device_id_type=MESH)
 
-    load = pltpu.make_async_copy(spectra_ref, spec, spec_sem)
-    load.start()
-
     def rows_of(block):
         return pl.ds(pl.multiple_of(block * BLK, BLK), BLK)
 
+    at = lax.broadcasted_iota(jnp.int32, (tsize, 4 * WCOLS), 1)
+    x = lax.broadcasted_iota(jnp.int32, (tsize, 4 * WCOLS), 0)
+    picked = (x == 4 * (at % WCOLS) + at // WCOLS) & (at % WCOLS < tsize // 4)
+    order[...] = jnp.where(picked, 1.0, 0.0).astype(jnp.bfloat16)
+
+    loads[0].wait()
+    n_left = length // BLK
+
     def left_body(a, carry):
         row = me * (band // BLK) + a
-        ca, sa = left_a[0, pl.ds(row, 1), :], left_a[1, pl.ds(row, 1), :]
-        cb, sb = left_b[0], left_b[1]
+        ca, sa = f384[0, pl.ds(row, 1), :], f384[1, pl.ds(row, 1), :]
+        cb, sb = f384[0, pl.ds(n_left, BLK), :], f384[1, pl.ds(n_left, BLK), :]
         left[0, rows_of(a), :] = (ca * cb - sa * sb).astype(jnp.bfloat16)
         left[1, rows_of(a), :] = (-(sa * cb + ca * sb)).astype(jnp.bfloat16)
         return carry
 
     lax.fori_loop(0, band // BLK, left_body, 0)
+    loads[1].wait()
 
     def tx_body(a, carry):
-        ca, sa = tx_a[0, pl.ds(a, 1), :], tx_a[1, pl.ds(a, 1), :]
-        cb, sb = tx_b[0], tx_b[1]
-        table_x[rows_of(a), :] = (ca * cb - sa * sb).astype(jnp.bfloat16)
-        table_x[rows_of(a + tsize // BLK), :] = (sa * cb + ca * sb).astype(jnp.bfloat16)
-        return carry
-
-    lax.fori_loop(0, tsize // BLK, tx_body, 0)
+        ca, sa = f512[0, pl.ds(a, 1), :], f512[1, pl.ds(a, 1), :]
+        for s in range(4):
+            where = pl.ds((s + 1) * BLK, BLK)
+            cb, sb = f512[0, where, :], f512[1, where, :]
+            table_x[s, rows_of(a), :] = (ca * cb - sa * sb).astype(jnp.bfloat16)
+            table_x[s, rows_of(a + WCOLS // BLK), :] = (sa * cb + ca * sb).astype(jnp.bfloat16)
+        return carry
+
+    lax.fori_loop(0, WCOLS // BLK, tx_body, 0)
+    loads[2].wait()
+    ft = kq // 2
 
     def te_body(a, carry):
-        ca, sa = te_a[0, pl.ds(a, 1), :], te_a[1, pl.ds(a, 1), :]
+        ca, sa = f256[0, pl.ds(a, 1), :], f256[1, pl.ds(a, 1), :]
+        per = ft // BLK
+        tile, u, block = a // per % 2, a // (2 * per), a % per
         for part in range(2):
-            cb, sb = te_b[part, 0], te_b[part, 1]
-            table_e[part, rows_of(a), :] = (ca * cb - sa * sb).astype(jnp.bfloat16)
+            where = pl.ds(n_left + part * BLK, BLK)
+            cb, sb = f256[0, where, :], f256[1, where, :]
+            row = (part * 4 + u) * ft + block * BLK
+            table_e[tile, pl.ds(pl.multiple_of(row, BLK), BLK), :] = (ca * cb - sa * sb).astype(
+                jnp.bfloat16
+            )
         return carry
 
     lax.fori_loop(0, length // BLK, te_body, 0)
+    pl.semaphore_wait(barrier, bands)
+    loads[4].wait()
+    loads[5].wait()
+
+    def orient_body(o, carry):
+        picture = bank[index_ref[core * share + o]].astype(jnp.float32)
+        centred = picture - jnp.mean(picture)
+        scale = lax.rsqrt(jnp.mean(centred * centred) + 1e-06)
+        template = (centred * scale).astype(jnp.bfloat16)
+        template = jnp.dot(template, order[...], preferred_element_type=jnp.float32)
+        template = template.astype(jnp.bfloat16)
+        for n in range(2):
+            value = jnp.dot(left[n], template, preferred_element_type=jnp.float32)
+            value = value.astype(jnp.bfloat16)
+            for s in range(4):
+                piece = value[:, s * WCOLS : (s + 1) * WCOLS]
+                if n == 0:
+                    rows_in[s, 0, :, pl.ds(0, WCOLS)] = piece
+                    rows_in[s, 1, :, pl.ds(WCOLS, WCOLS)] = -piece
+                else:
+                    rows_in[s, 0, :, pl.ds(WCOLS, WCOLS)] = piece
+                    rows_in[s, 1, :, pl.ds(0, WCOLS)] = piece
+
+        def half_body(h, inner):
+            rows = pl.ds(pl.multiple_of(h * hb, hb), hb)
+            total = None
+            for tile in range(2):
+                cols = pl.ds(tile * ft, ft)
+                re, im = [], []
+                for s in range(4):
+                    wide = table_x[s, :, cols]
+                    re.append(jnp.dot(rows_in[s, 0, rows, :], wide, preferred_element_type=jnp.float32))
+                    im.append(jnp.dot(rows_in[s, 1, rows, :], wide, preferred_element_type=jnp.float32))
+                s02r, d02r, s13r, d13r = re[0] + re[2], re[0] - re[2], re[1] + re[3], re[1] - re[3]
+                s02i, d02i, s13i, d13i = im[0] + im[2], im[0] - im[2], im[1] + im[3], im[1] - im[3]
+                quads = [
+                    (s02r + s13r, s02i + s13i),
+                    (d02r + d13i, d02i - d13r),
+                    (s02r - s13r, s02i - s13i),
+                    (d02r - d13i, d02i + d13r),
+                ]
+                for u, (t_re, t_im) in enumerate(quads):
+                    t_re = t_re.astype(jnp.bfloat16).astype(PRODUCT)
+                    t_im = t_im.astype(jnp.bfloat16).astype(PRODUCT)
+                    where = pl.ds(u * kq + tile * ft, ft)
+                    for m in range(2):
+                        m_re = spec[m, 0, rows, where].astype(PRODUCT)
+                        m_im = spec[m, 1, rows, where].astype(PRODUCT)
+                        p_re = (m_re * t_re + m_im * t_im).astype(jnp.bfloat16)
+                        p_im = (m_im * t_re - m_re * t_im).astype(jnp.bfloat16)
+                        prod[tile, pl.ds(m * hb, hb), pl.ds(u * ft, ft)] = p_re
+                        prod[tile, pl.ds(m * hb, hb), pl.ds((4 + u) * ft, ft)] = p_im
+                value = jnp.dot(prod[tile], table_e[tile], preferred_element_type=jnp.float32)
+                total = value if total is None else total + value
+            total = total.astype(jnp.bfloat16)
+            for d in range(bands):
+                m, xh = d // 2, d % 2
+                tile = total[m * hb : (m + 1) * hb, xh * WCOLS : (xh + 1) * WCOLS]
+
+                @pl.when(me == d)
+                def _():
+                    recv[me, o, rows, :] = tile
+
+                @pl.when(me != d)
+                def _():
+                    send[d, o, rows, :] = tile
+
+            for k in (2, 1, 3):
+                part_copy(k, lax.rem(me + k, bands), me, o, h).start()
+            return inner
+
+        lax.fori_loop(0, 2, half_body, 0)
+        return carry
+
+    def part_copy(k, dest, source, o, h):
+        rows = pl.ds(pl.multiple_of(h * hb, hb), hb)
+        return pltpu.make_async_remote_copy(
+            src_ref=send.at[dest, o, rows, :], dst_ref=recv.at[source, o, rows, :],
+            send_sem=send_sem.at[k, o, h], recv_sem=recv_sem.at[source, o, h],
+            device_id={"row": dest}, device_id_type=MESH,
+        )
+
+    lax.fori_loop(0, share, orient_body, 0)
+    loads[3].wait()
+    n_col = band // BLK
 
     def col_body(a, carry):
-        ca, sa = col_a[0, pl.ds(a, 1), :], col_a[1, pl.ds(a, 1), :]
-        value = ca * col_b[0] - sa * col_b[1]
+        ca, sa = f1024[0, pl.ds(a, 1), :], f1024[1, pl.ds(a, 1), :]
+        value = ca * f1024[0, pl.ds(n_col, BLK), :] - sa * f1024[1, pl.ds(n_col, BLK), :]
         high = value.astype(jnp.bfloat16)
         col_hi[rows_of(a), :] = high
         col_lo[rows_of(a), :] = (value - high.astype(jnp.float32)).astype(jnp.bfloat16)
-        ta, ua = tw_a[0, pl.ds(a, 1), :], tw_a[1, pl.ds(a, 1), :]
-        tb, ub = tw_b[0], tw_b[1]
+        base = n_left + BLK
+        ta, ua = f384[0, pl.ds(base + a, 1), :], f384[1, pl.ds(base + a, 1), :]
+        where = pl.ds(base + n_col, BLK)
+        tb, ub = f384[0, where, :], f384[1, where, :]
         lane = lax.broadcasted_iota(jnp.int32, (BLK, 3 * WCOLS), 1) % WCOLS
         twc[rows_of(a), :] = ta * tb - ua * ub
         sine = ua * tb + ta * ub
@@ -210,66 +325,6 @@
 
     lax.fori_loop(0, band // BLK, col_body, 0)
 
-    pl.semaphore_wait(barrier, bands)
-    load.wait()
-
-    kt = 256
-
-    def orient_body(o, carry):
-        picture = bank_ref[index_ref[core * share + o]].astype(jnp.float32)
-        centred = picture - jnp.mean(picture)
-        scale = lax.rsqrt(jnp.mean(centred * centred) + 1e-06)
-        template = (centred * scale).astype(jnp.bfloat16)
-        pass_re = jnp.dot(left[0], template, preferred_element_type=jnp.float32)
-        pass_im = jnp.dot(left[1], template, preferred_element_type=jnp.float32)
-        pass_re = pass_re.astype(jnp.bfloat16)
-        pass_im = pass_im.astype(jnp.bfloat16)
-        rows_in[0, :, pl.ds(0, tsize)] = pass_re
-        rows_in[0, :, pl.ds(tsize, tsize)] = pass_im
-        rows_in[1, :, pl.ds(0, tsize)] = pass_im
-        rows_in[1, :, pl.ds(tsize, tsize)] = -pass_re
-        acc[...] = jnp.zeros_like(acc)
-
-        def kx_body(k, inner):
-            cols = pl.ds(pl.multiple_of(k * kt, kt), kt)
-            wide = table_x[:, cols]
-            t_re = jnp.dot(rows_in[0], wide, preferred_element_type=jnp.float32)
-            t_im = jnp.dot(rows_in[1], wide, preferred_element_type=jnp.float32)
-            t_re = t_re.astype(jnp.bfloat16).astype(jnp.float32)
-            t_im = t_im.astype(jnp.bfloat16).astype(jnp.float32)
-            for m in range(2):
-                m_re = spec[m, 0, :, cols].astype(jnp.float32)
-                m_im = spec[m, 1, :, cols].astype(jnp.float32)
-                p_re = (m_re * t_re + m_im * t_im).astype(jnp.bfloat16)
-                p_im = (m_im * t_re - m_re * t_im).astype(jnp.bfloat16)
-                acc[m] += jnp.dot(
-                    p_re, table_e[0, cols, :], preferred_element_type=jnp.float32
-                ) + jnp.dot(p_im, table_e[1, cols, :], preferred_element_type=jnp.float32)
-            return inner
-
-        lax.fori_loop(0, length // kt, kx_body, 0)
-        for d in range(bands):
-            tile = acc[d // 2, :, pl.ds(d % 2 * WCOLS, WCOLS)].astype(jnp.bfloat16)
-
-            @pl.when(me == d)
-            def _():
-                recv[me, o] = tile
-
-            @pl.when(me != d)
-            def _():
-                send[d, o] = tile
-
-        for k in (2, 1, 3):
-            dest = lax.rem(me + k, bands)
-            pltpu.make_async_remote_copy(
-                src_ref=send.at[dest, o], dst_ref=recv.at[me, o],
-                send_sem=send_sem.at[k, o], recv_sem=recv_sem.at[me, o],
-                device_id={"row": dest}, device_id_type=MESH,
-            ).start()
-        return carry
-
-    lax.fori_loop(0, share, orient_body, 0)
-
     peak[...] = jnp.full_like(peak, -1e30)
     power[...] = jnp.zeros_like(power)
     factor = 1.0 / (length * tsize)
@@ -278,11 +333,8 @@
     def column_body(o, carry):
         for k in range(1, bands):
             source = lax.rem(me + k, bands)
-            pltpu.make_async_remote_copy(
-                src_ref=send.at[source, o], dst_ref=recv.at[source, o],
-                send_sem=send_sem.at[k, o], recv_sem=recv_sem.at[source, o],
-                device_id={"row": source}, device_id_type=MESH,
-            ).wait_recv()
+            for h in range(2):
+                part_copy(k, source, source, o, h).wait_recv()
 
         def chunk(c, inner):
             rows = pl.ds(pl.multiple_of(c * rc, rc), rc)
@@ -330,7 +382,6 @@
         else:
             own[q] = jnp.where(first, pltpu.roll(hi, half, 1), po)
 
-    hb = band // 2
     mine = pl.ds(pl.multiple_of(core * hb, hb), hb)
     theirs = pl.ds(pl.multiple_of((1 - core) * hb, hb), hb)
     swap = pltpu.make_async_remote_copy(
@@ -343,7 +394,7 @@
     first = lax.broadcasted_iota(jnp.int32, (hb, WCOLS), 1) < half
     for q in range(4):
         one, two = own[q, mine, :], sibling[q]
-        total = jnp.where(first, jnp.maximum(one, two), one + two)
+        total = jnp.where(first, jnp.maximum(one, two), one + two).astype(final.dtype)
 
         @pl.when(me == q)
         def _():
@@ -377,12 +428,6 @@
         forward(source, mine).start()
     for source in range(4):
         forward(source, theirs).wait_recv()
-    first = lax.broadcasted_iota(jnp.int32, (band, WCOLS), 1) < half
-    for m in range(2):
-        a, b = final[2 * m], final[2 * m + 1]
-        peak_ref[m, 0] = jnp.where(first, a, pltpu.roll(b, half, 1))
-        power_ref[m, 0] = jnp.where(first, pltpu.roll(a, half, 1), b)
-
     for source in range(4):
         forward(source, mine).wait_send()
     for k in range(1, bands):
@@ -391,14 +436,20 @@
     def drain(o, carry):
         for k in range(1, bands):
             dest = lax.rem(me + k, bands)
-            pltpu.make_async_remote_copy(
-                src_ref=send.at[dest, o], dst_ref=recv.at[me, o],
-                send_sem=send_sem.at[k, o], recv_sem=recv_sem.at[me, o],
-                device_id={"row": dest}, device_id_type=MESH,
-            ).wait_send()
+            for h in range(2):
+                part_copy(k, dest, me, o, h).wait_send()
         return carry
 
     lax.fori_loop(0, share, drain, 0)
+
+
+def assemble_kernel(maps, peak_ref, power_ref):
+    half = WCOLS // 2
+    first = lax.broadcasted_iota(jnp.int32, maps.shape[1:], 1) < half
+    for m in range(2):
+        a, b = maps[2 * m].astype(jnp.float32), maps[2 * m + 1].astype(jnp.float32)
+        peak_ref[m, 0] = jnp.where(first, a, pltpu.roll(b, half, 1))
+        power_ref[m, 0] = jnp.where(first, pltpu.roll(a, half, 1), b)
 
 
 def shards_fused(spectra, bank, orient_index):
@@ -412,56 +463,64 @@
 
     small = np.arange(BLK)
     y = np.arange(tsize)
-    kx = np.arange(length)
+    kq = np.arange(length // 4)
     lane = np.arange(2 * WCOLS)
     lane_x = lane // WCOLS * half + lane % half
     is_im = lane % WCOLS >= half
     quarter = two_pi / 4
-    te_b = np.stack(
-        [
-            factors(small, lane_x, length, np.where(is_im, -quarter, 0.0)),
-            factors(small, lane_x, length, np.where(is_im, 0.0, quarter)),
-        ]
-    )
+    steps = np.arange(length // BLK) * BLK
+    short = np.arange(band // BLK) * BLK
     j = np.arange(band)
     col_j = np.concatenate([j, j])
     col_shift = np.where(np.arange(2 * band) < band, 0.0, quarter)
     rho = np.repeat(np.arange(1, 4), WCOLS)
-    tables = [
-        factors(np.arange(length // BLK) * BLK, y, length),
-        factors(small, y, length),
-        factors(np.arange(tsize // BLK) * BLK, kx, length),
-        factors(small, kx, length),
-        factors(np.arange(length // BLK) * BLK, lane_x, length),
-        te_b,
-        factors(np.arange(band // BLK) * BLK, col_j, band),
-        factors(small, col_j, band, col_shift),
-        factors(np.arange(band // BLK) * BLK, rho, length),
-        factors(small, rho, length),
-    ]
-    out = jax.ShapeDtypeStruct((2, 1, band, WCOLS), f32)
+    spread = np.concatenate([np.arange(BLK) * 4 * BLK] + [4 * small + s for s in range(4)])
+    w384 = np.concatenate(
+        [
+            factors(steps, y, length),
+            factors(small, y, length),
+            factors(short, rho, length),
+            factors(small, rho, length),
+        ],
+        1,
+    )
+    w512 = factors(spread, kq, length)
+    w256 = np.concatenate(
+        [
+            factors(steps, lane_x, length),
+            factors(small, lane_x, length, np.where(is_im, -quarter, 0.0)),
+            factors(small, lane_x, length, np.where(is_im, 0.0, quarter)),
+        ],
+        1,
+    )
+    w1024 = np.concatenate(
+        [factors(short, col_j, band), factors(small, col_j, band, col_shift)], 1
+    )
+    tables = [w384, w512, w256, w1024]
     vmem = pl.BlockSpec(memory_space=pltpu.VMEM)
+    hbm = pl.BlockSpec(memory_space=pl.ANY)
     dma = pltpu.SemaphoreType.DMA
-    return pl.pallas_call(
+    maps = pl.pallas_call(
         functools.partial(fused_kernel, (bands, share, band, length, tsize)),
-        out_shape=(out, out),
-        in_specs=[
-            pl.BlockSpec(memory_space=pltpu.SMEM),
-            pl.BlockSpec(memory_space=pl.ANY),
+        out_shape=jax.ShapeDtypeStruct((4, band, WCOLS), MAPS),
+        in_specs=[pl.BlockSpec(memory_space=pltpu.SMEM)] + [hbm] * (2 + len(tables)),
+        out_specs=vmem,
+        scratch_shapes=[
+            pltpu.VMEM(spectra.shape, bf),
+            pltpu.VMEM(bank.shape, bf),
         ]
-        + [vmem] * (1 + len(tables)),
-        out_specs=(vmem, vmem),
-        scratch_shapes=[
-            pltpu.VMEM((2, 2, band, length), bf),
+        + [pltpu.VMEM(table.shape, f32) for table in tables]
+        + [
             pltpu.VMEM((2, band, tsize), bf),
-            pltpu.VMEM((2 * tsize, length), bf),
+            pltpu.VMEM((4, 2 * WCOLS, length // 4), bf),
             pltpu.VMEM((2, length, 2 * WCOLS), bf),
             pltpu.VMEM((band, 2 * band), bf),
             pltpu.VMEM((band, 2 * band), bf),
             pltpu.VMEM((band, 3 * WCOLS), f32),
             pltpu.VMEM((band, 3 * WCOLS), f32),
-            pltpu.VMEM((2, band, 2 * tsize), bf),
-            pltpu.VMEM((2, band, 2 * WCOLS), f32),
+            pltpu.VMEM((tsize, 4 * WCOLS), bf),
+            pltpu.VMEM((4, 2, band, 2 * WCOLS), bf),
+            pltpu.VMEM((2, band, length), bf),
             pltpu.VMEM((bands, share, band, WCOLS), bf),
             pltpu.VMEM((bands, share, band, WCOLS), bf),
             pltpu.VMEM((2 * band, 2 * WCOLS), bf),
@@ -470,11 +529,10 @@
             pltpu.VMEM((band, 2 * WCOLS), f32),
             pltpu.VMEM((4, band, WCOLS), f32),
             pltpu.VMEM((4, band // 2, WCOLS), f32),
-            pltpu.VMEM((4, band // 2, WCOLS), f32),
-            pltpu.VMEM((4, band, WCOLS), f32),
-            dma,
-            dma((bands, share)),
-            dma((bands, share)),
+            pltpu.VMEM((4, band // 2, WCOLS), MAPS),
+            dma((6,)),
+            dma((bands, share, 2)),
+            dma((bands, share, 2)),
             dma,
             dma,
             dma((bands,)),
@@ -483,9 +541,13 @@
             dma((bands,)),
         ],
         compiler_params=pltpu.CompilerParams(
-            collective_id=0, has_side_effects=True, vmem_limit_bytes=60 << 20
+            collective_id=0, has_side_effects=True, vmem_limit_bytes=58 << 20
         ),
     )(orient_index, spectra, bank, *tables)
+    out = jax.ShapeDtypeStruct((2, 1, band, WCOLS), f32)
+    return pl.pallas_call(
+        assemble_kernel, out_shape=(out, out), in_specs=[vmem], out_specs=(vmem, vmem)
+    )(maps)
 
 
 def shards(spectra, bank, orient_index):
@@ -494,6 +556,7 @@
         and lax.axis_size("orient") == 2
         and spectra.shape[0] == 2
         and spectra.shape[2] % 128 == 0
+        and bank.shape[1] == 3 * WCOLS
         and spectra.shape[3] == 4 * spectra.shape[2]
     )
     body = shards_fused if fits else shards_general

time: 87.6 us -> 75.7 us (0.86)
  Pallas kernels: 82.9 us -> 74.9 us
  local copies, waits for them, and re-layouts: 3.74 us -> 0 us
    pallas_call x1, Pallas kernels: 82.9 us -> 72.7 us  [shards_fused(): pl.pallas_call(functools.partial(fused_kernel, (bands, share, band, lengt...]
    unnamed x2 -> x0, local copies, waits for them, and re-layouts: 3.74 us -> none
    pallas_call x0 -> x1, Pallas kernels: none -> 2.19 us  [shards_fused(): pl.pallas_call(assemble_kernel, out_shape=(out, out), in_specs=[vmem], ou...]
where the time goes in v2:
time: 75.7 us; the launch traced here: 75.5 us
  Pallas kernels  74.9 us (99%)
    pallas_call x1, Pallas kernels, shards_fused(): pl.pallas_call(functools.partial(fused_kernel, (bands, share, band, lengt...  72.7 us
    pallas_call x1, Pallas kernels, shards_fused(): pl.pallas_call(assemble_kernel, out_shape=(out, out), in_specs=[vmem], ou...  2.19 us

profile of v2, /device:TPU:0, one launch (start us, length us, event | category | flops | bytes accessed | tf_op | source)
XLA Modules:
  0.0 75.5 jit_solution(15299264466272395223)
XLA Ops:
  0.6 72.7 %shard_map.86.maps = bf16[4,512,128]{2,1,0:T(8,128)(2,1)} custom-call(s32[8]{0:T(128)} %index_ref.1, bf16[2,2,512,2048]{3,2,1,0:T(8,128)(2,1)} %spectra_ref.1, bf16[8,384,384]{2,1,0:T(8,128)(2,1)} %bank_ref.1, f32[2,192,384]{2,1,0:T(8,128)} %constant.8.clone.w384, f32[2,80,512]{2,1,0:T(8,128)} %constant.9.clone.w512, f32[2,160,256]{2,1,0:T(8,128)} %constant.10.clone.w256, ...), custom_call_target="tpu_custom_call" | custom-call | tf_op jit(solution)/shard_map/pallas_call | solution.py:503
  73.3 2.2 %shard_map.87 = (f32[2,1,512,128]{3,2,1,0:T(8,128)}, f32[2,1,512,128]{3,2,1,0:T(8,128)}) custom-call(bf16[4,512,128]{2,1,0:T(8,128)(2,1)} %shard_map.86.maps), custom_call_target="tpu_custom_call" | custom-call | tf_op jit(solution)/shard_map/pallas_call | solution.py:548

commit v3 on v2

--- a/solution.py
+++ b/solution.py
@@ -14,6 +14,7 @@
 BLK = 16
 PRODUCT = jnp.float32
 MAPS = jnp.bfloat16
+PARTS = 4
 
 
 two_pi = 2.0 * math.pi
@@ -145,7 +146,7 @@
     final,
     spec, bank, f384, f512, f256, f1024,
     left, table_x, table_e, col_hi, col_lo, twc, tws, order,
-    rows_in, prod, send, recv, v_hi, v_lo, peak, power,
+    rows_in, prod, send, recv, v_hi, v_lo, corr_acc, peak, power,
     own, sibling, merged,
     load_sem, send_sem, recv_sem, pair_send, pair_recv,
     map_send, map_recv, fwd_send, fwd_recv,
@@ -153,6 +154,7 @@
     bands, share, band, length, tsize = sizes
     half = WCOLS // 2
     hb = band // 2
+    pb = band // PARTS
     kq = length // 4
     me = lax.axis_index("row")
     core = lax.axis_index("orient")
@@ -183,15 +185,17 @@
     loads[0].wait()
     n_left = length // BLK
 
-    def left_body(a, carry):
-        row = me * (band // BLK) + a
-        ca, sa = f384[0, pl.ds(row, 1), :], f384[1, pl.ds(row, 1), :]
+    def left_body(group, carry):
         cb, sb = f384[0, pl.ds(n_left, BLK), :], f384[1, pl.ds(n_left, BLK), :]
-        left[0, rows_of(a), :] = (ca * cb - sa * sb).astype(jnp.bfloat16)
-        left[1, rows_of(a), :] = (-(sa * cb + ca * sb)).astype(jnp.bfloat16)
-        return carry
-
-    lax.fori_loop(0, band // BLK, left_body, 0)
+        for block in range(8):
+            a = group * 8 + block
+            row = me * (band // BLK) + a
+            ca, sa = f384[0, pl.ds(row, 1), :], f384[1, pl.ds(row, 1), :]
+            left[0, rows_of(a), :] = (ca * cb - sa * sb).astype(jnp.bfloat16)
+            left[1, rows_of(a), :] = (-(sa * cb + ca * sb)).astype(jnp.bfloat16)
+        return carry
+
+    lax.fori_loop(0, band // BLK // 8, left_body, 0)
     loads[1].wait()
 
     def tx_body(a, carry):
@@ -207,23 +211,24 @@
     loads[2].wait()
     ft = kq // 2
 
-    def te_body(a, carry):
-        ca, sa = f256[0, pl.ds(a, 1), :], f256[1, pl.ds(a, 1), :]
+    def te_body(group, carry):
         per = ft // BLK
-        tile, u, block = a // per % 2, a // (2 * per), a % per
-        for part in range(2):
-            where = pl.ds(n_left + part * BLK, BLK)
-            cb, sb = f256[0, where, :], f256[1, where, :]
-            row = (part * 4 + u) * ft + block * BLK
-            table_e[tile, pl.ds(pl.multiple_of(row, BLK), BLK), :] = (ca * cb - sa * sb).astype(
-                jnp.bfloat16
-            )
-        return carry
-
-    lax.fori_loop(0, length // BLK, te_body, 0)
+        tile, u = group % 2, group // 2
+        cb = [f256[0, pl.ds(n_left + part * BLK, BLK), :] for part in range(2)]
+        sb = [f256[1, pl.ds(n_left + part * BLK, BLK), :] for part in range(2)]
+        for block in range(per):
+            a = group * per + block
+            ca, sa = f256[0, pl.ds(a, 1), :], f256[1, pl.ds(a, 1), :]
+            for part in range(2):
+                row = (part * 4 + u) * ft + block * BLK
+                table_e[tile, pl.ds(pl.multiple_of(row, BLK), BLK), :] = (
+                    ca * cb[part] - sa * sb[part]
+                ).astype(jnp.bfloat16)
+        return carry
+
+    lax.fori_loop(0, 8, te_body, 0)
     pl.semaphore_wait(barrier, bands)
     loads[4].wait()
-    loads[5].wait()
 
     def orient_body(o, carry):
         picture = bank[index_ref[core * share + o]].astype(jnp.float32)
@@ -244,8 +249,12 @@
                     rows_in[s, 0, :, pl.ds(WCOLS, WCOLS)] = piece
                     rows_in[s, 1, :, pl.ds(0, WCOLS)] = piece
 
-        def half_body(h, inner):
-            rows = pl.ds(pl.multiple_of(h * hb, hb), hb)
+        @pl.when(o == 0)
+        def _():
+            loads[5].wait()
+
+        def part_body(h, inner):
+            rows = pl.ds(pl.multiple_of(h * pb, pb), pb)
             total = None
             for tile in range(2):
                 cols = pl.ds(tile * ft, ft)
@@ -271,14 +280,14 @@
                         m_im = spec[m, 1, rows, where].astype(PRODUCT)
                         p_re = (m_re * t_re + m_im * t_im).astype(jnp.bfloat16)
                         p_im = (m_im * t_re - m_re * t_im).astype(jnp.bfloat16)
-                        prod[tile, pl.ds(m * hb, hb), pl.ds(u * ft, ft)] = p_re
-                        prod[tile, pl.ds(m * hb, hb), pl.ds((4 + u) * ft, ft)] = p_im
+                        prod[tile, pl.ds(m * pb, pb), pl.ds(u * ft, ft)] = p_re
+                        prod[tile, pl.ds(m * pb, pb), pl.ds((4 + u) * ft, ft)] = p_im
                 value = jnp.dot(prod[tile], table_e[tile], preferred_element_type=jnp.float32)
                 total = value if total is None else total + value
             total = total.astype(jnp.bfloat16)
             for d in range(bands):
                 m, xh = d // 2, d % 2
-                tile = total[m * hb : (m + 1) * hb, xh * WCOLS : (xh + 1) * WCOLS]
+                tile = total[m * pb : (m + 1) * pb, xh * WCOLS : (xh + 1) * WCOLS]
 
                 @pl.when(me == d)
                 def _():
@@ -292,11 +301,11 @@
                 part_copy(k, lax.rem(me + k, bands), me, o, h).start()
             return inner
 
-        lax.fori_loop(0, 2, half_body, 0)
+        lax.fori_loop(0, PARTS, part_body, 0)
         return carry
 
     def part_copy(k, dest, source, o, h):
-        rows = pl.ds(pl.multiple_of(h * hb, hb), hb)
+        rows = pl.ds(pl.multiple_of(h * pb, pb), pb)
         return pltpu.make_async_remote_copy(
             src_ref=send.at[dest, o, rows, :], dst_ref=recv.at[source, o, rows, :],
             send_sem=send_sem.at[k, o, h], recv_sem=recv_sem.at[source, o, h],
@@ -331,41 +340,47 @@
     rc = 64
 
     def column_body(o, carry):
-        for k in range(1, bands):
-            source = lax.rem(me + k, bands)
-            for h in range(2):
+        corr_acc[...] = jnp.zeros_like(corr_acc)
+
+        def part_column(h, inner):
+            for k in range(1, bands):
+                source = lax.rem(me + k, bands)
                 part_copy(k, source, source, o, h).wait_recv()
-
-        def chunk(c, inner):
-            rows = pl.ds(pl.multiple_of(c * rc, rc), rc)
-            lane = lax.broadcasted_iota(jnp.int32, (rc, WCOLS), 1)
-            first = lane < half
-            b0, b1, b2, b3 = [recv[b, o, rows, :].astype(jnp.float32) for b in range(4)]
-            s02, d02, s13, d13 = b0 + b2, b0 - b2, b1 + b3, b1 - b3
-            turned = pltpu.roll(d13, half, 1)
-            turned = jnp.where(first, -turned, turned)
-            u = [s02 + s13, d02 + turned, s02 - s13, d02 - turned]
-            v = [u[0]]
-            for rho in range(1, 4):
-                span = pl.ds((rho - 1) * WCOLS, WCOLS)
-                v.append(u[rho] * twc[rows, span] + pltpu.roll(u[rho], half, 1) * tws[rows, span])
-            for pair in range(2):
-                even, odd = v[2 * pair], v[2 * pair + 1]
-                v_re = jnp.where(first, even, pltpu.roll(odd, half, 1))
-                v_im = jnp.where(first, pltpu.roll(even, half, 1), odd)
-                span = pl.ds(pair * WCOLS, WCOLS)
-                for part, value in enumerate((v_re, v_im)):
-                    high = value.astype(jnp.bfloat16)
-                    where = pl.ds(pl.multiple_of(part * band + c * rc, rc), rc)
-                    v_hi[where, span] = high
-                    v_lo[where, span] = (value - high.astype(jnp.float32)).astype(jnp.bfloat16)
+            for c in range(pb // rc):
+                rows = pl.ds(pl.multiple_of(h * pb + c * rc, rc), rc)
+                lane = lax.broadcasted_iota(jnp.int32, (rc, WCOLS), 1)
+                first = lane < half
+                b0, b1, b2, b3 = [recv[b, o, rows, :].astype(jnp.float32) for b in range(4)]
+                s02, d02, s13, d13 = b0 + b2, b0 - b2, b1 + b3, b1 - b3
+                turned = pltpu.roll(d13, half, 1)
+                turned = jnp.where(first, -turned, turned)
+                u = [s02 + s13, d02 + turned, s02 - s13, d02 - turned]
+                v = [u[0]]
+                for rho in range(1, 4):
+                    span = pl.ds((rho - 1) * WCOLS, WCOLS)
+                    v.append(
+                        u[rho] * twc[rows, span] + pltpu.roll(u[rho], half, 1) * tws[rows, span]
+                    )
+                for pair in range(2):
+                    even, odd = v[2 * pair], v[2 * pair + 1]
+                    v_re = jnp.where(first, even, pltpu.roll(odd, half, 1))
+                    v_im = jnp.where(first, pltpu.roll(even, half, 1), odd)
+                    span = pl.ds(pair * WCOLS, WCOLS)
+                    for part, value in enumerate((v_re, v_im)):
+                        high = value.astype(jnp.bfloat16)
+                        where = pl.ds(part * pb + c * rc, rc)
+                        v_hi[where, span] = high
+                        v_lo[where, span] = (value - high.astype(jnp.float32)).astype(jnp.bfloat16)
+            cols = pl.ds(pl.multiple_of(h * 2 * pb, 2 * pb), 2 * pb)
+            high, low = col_hi[:, cols], col_lo[:, cols]
+            corr = jnp.dot(high, v_hi[...], preferred_element_type=jnp.float32)
+            corr += jnp.dot(low, v_hi[...], preferred_element_type=jnp.float32)
+            corr += jnp.dot(high, v_lo[...], preferred_element_type=jnp.float32)
+            corr_acc[...] += corr
             return inner
 
-        lax.fori_loop(0, band // rc, chunk, 0)
-        corr = jnp.dot(col_hi[...], v_hi[...], preferred_element_type=jnp.float32)
-        corr += jnp.dot(col_lo[...], v_hi[...], preferred_element_type=jnp.float32)
-        corr += jnp.dot(col_hi[...], v_lo[...], preferred_element_type=jnp.float32)
-        corr = corr * factor
+        lax.fori_loop(0, PARTS, part_column, 0)
+        corr = corr_acc[...] * factor
         peak[...] = jnp.maximum(peak[...], corr)
         power[...] += corr * corr
         return carry
@@ -384,25 +399,17 @@
 
     mine = pl.ds(pl.multiple_of(core * hb, hb), hb)
     theirs = pl.ds(pl.multiple_of((1 - core) * hb, hb), hb)
-    swap = pltpu.make_async_remote_copy(
-        src_ref=own.at[:, theirs, :], dst_ref=sibling,
-        send_sem=pair_send, recv_sem=pair_recv,
-        device_id={"orient": 1 - core}, device_id_type=MESH,
-    )
-    swap.start()
-    swap.wait()
+    def swap(k):
+        q = lax.rem(me + k, bands)
+        return pltpu.make_async_remote_copy(
+            src_ref=own.at[q, theirs, :], dst_ref=sibling.at[q],
+            send_sem=pair_send.at[k], recv_sem=pair_recv.at[k],
+            device_id={"orient": 1 - core}, device_id_type=MESH,
+        )
+
+    for k in (2, 1, 3, 0):
+        swap(k).start()
     first = lax.broadcasted_iota(jnp.int32, (hb, WCOLS), 1) < half
-    for q in range(4):
-        one, two = own[q, mine, :], sibling[q]
-        total = jnp.where(first, jnp.maximum(one, two), one + two).astype(final.dtype)
-
-        @pl.when(me == q)
-        def _():
-            final[me, mine, :] = total
-
-        @pl.when(me != q)
-        def _():
-            merged[q] = total
 
     def map_copy(k, source):
         dest = lax.rem(me + k, bands)
@@ -419,8 +426,16 @@
             device_id={"orient": 1 - core}, device_id_type=MESH,
         )
 
-    for k in (2, 1, 3):
-        map_copy(k, me).start()
+    for k in (2, 1, 3, 0):
+        swap(k).wait_recv()
+        q = lax.rem(me + k, bands)
+        one, two = own[q, mine, :], sibling[q]
+        total = jnp.where(first, jnp.maximum(one, two), one + two).astype(final.dtype)
+        if k == 0:
+            final[me, mine, :] = total
+        else:
+            merged[q] = total
+            map_copy(k, me).start()
     forward(me, mine).start()
     for k in (1, 3, 2):
         source = lax.rem(me + k, bands)
@@ -432,11 +447,13 @@
         forward(source, mine).wait_send()
     for k in range(1, bands):
         map_copy(k, me).wait_send()
+    for k in range(bands):
+        swap(k).wait_send()
 
     def drain(o, carry):
         for k in range(1, bands):
             dest = lax.rem(me + k, bands)
-            for h in range(2):
+            for h in range(PARTS):
                 part_copy(k, dest, me, o, h).wait_send()
         return carry
 
@@ -470,9 +487,10 @@
     quarter = two_pi / 4
     steps = np.arange(length // BLK) * BLK
     short = np.arange(band // BLK) * BLK
-    j = np.arange(band)
-    col_j = np.concatenate([j, j])
-    col_shift = np.where(np.arange(2 * band) < band, 0.0, quarter)
+    pb = band // PARTS
+    at = np.arange(2 * band)
+    col_j = at // (2 * pb) * pb + at % pb
+    col_shift = np.where(at // pb % 2 == 0, 0.0, quarter)
     rho = np.repeat(np.arange(1, 4), WCOLS)
     spread = np.concatenate([np.arange(BLK) * 4 * BLK] + [4 * small + s for s in range(4)])
     w384 = np.concatenate(
@@ -520,21 +538,22 @@
             pltpu.VMEM((band, 3 * WCOLS), f32),
             pltpu.VMEM((tsize, 4 * WCOLS), bf),
             pltpu.VMEM((4, 2, band, 2 * WCOLS), bf),
-            pltpu.VMEM((2, band, length), bf),
+            pltpu.VMEM((2, 2 * band // PARTS, length), bf),
             pltpu.VMEM((bands, share, band, WCOLS), bf),
             pltpu.VMEM((bands, share, band, WCOLS), bf),
-            pltpu.VMEM((2 * band, 2 * WCOLS), bf),
-            pltpu.VMEM((2 * band, 2 * WCOLS), bf),
+            pltpu.VMEM((2 * band // PARTS, 2 * WCOLS), bf),
+            pltpu.VMEM((2 * band // PARTS, 2 * WCOLS), bf),
+            pltpu.VMEM((band, 2 * WCOLS), f32),
             pltpu.VMEM((band, 2 * WCOLS), f32),
             pltpu.VMEM((band, 2 * WCOLS), f32),
             pltpu.VMEM((4, band, WCOLS), f32),
             pltpu.VMEM((4, band // 2, WCOLS), f32),
             pltpu.VMEM((4, band // 2, WCOLS), MAPS),
             dma((6,)),
-            dma((bands, share, 2)),
-            dma((bands, share, 2)),
-            dma,
-            dma,
+            dma((bands, share, PARTS)),
+            dma((bands, share, PARTS)),
+            dma((bands,)),
+            dma((bands,)),
             dma((bands,)),
             dma((bands,)),
             dma((bands,)),

time: 75.7 us -> 70.3 us (0.929)
  Pallas kernels: 74.9 us -> 69.4 us
    pallas_call x1, Pallas kernels: 72.7 us -> 67.2 us  [shards_fused(): pl.pallas_call(functools.partial(fused_kernel, (bands, share, band, lengt...]
where the time goes in v3:
time: 70.3 us; the launch traced here: 70.1 us
  Pallas kernels  69.4 us (99%)
    pallas_call x1, Pallas kernels, shards_fused(): pl.pallas_call(functools.partial(fused_kernel, (bands, share, band, lengt...  67.2 us
    pallas_call x1, Pallas kernels, shards_fused(): pl.pallas_call(assemble_kernel, out_shape=(out, out), in_specs=[vmem], ou...  2.19 us

profile of v3, /device:TPU:0, one launch (start us, length us, event | category | flops | bytes accessed | tf_op | source)
XLA Modules:
  0.0 70.1 jit_solution(4807662449282384777)
XLA Ops:
  0.6 67.2 %shard_map.86.maps = bf16[4,512,128]{2,1,0:T(8,128)(2,1)} custom-call(s32[8]{0:T(128)} %index_ref.1, bf16[2,2,512,2048]{3,2,1,0:T(8,128)(2,1)} %spectra_ref.1, bf16[8,384,384]{2,1,0:T(8,128)(2,1)} %bank_ref.1, f32[2,192,384]{2,1,0:T(8,128)} %constant.8.clone.w384, f32[2,80,512]{2,1,0:T(8,128)} %constant.9.clone.w512, f32[2,160,256]{2,1,0:T(8,128)} %constant.10.clone.w256, ...), custom_call_target="tpu_custom_call" | custom-call | tf_op jit(solution)/shard_map/pallas_call | solution.py:521
  67.9 2.2 %shard_map.87 = (f32[2,1,512,128]{3,2,1,0:T(8,128)}, f32[2,1,512,128]{3,2,1,0:T(8,128)}) custom-call(bf16[4,512,128]{2,1,0:T(8,128)(2,1)} %shard_map.86.maps), custom_call_target="tpu_custom_call" | custom-call | tf_op jit(solution)/shard_map/pallas_call | solution.py:567

commit v4 on v3

--- a/solution.py
+++ b/solution.py
@@ -463,10 +463,9 @@
 def assemble_kernel(maps, peak_ref, power_ref):
     half = WCOLS // 2
     first = lax.broadcasted_iota(jnp.int32, maps.shape[1:], 1) < half
-    for m in range(2):
-        a, b = maps[2 * m].astype(jnp.float32), maps[2 * m + 1].astype(jnp.float32)
-        peak_ref[m, 0] = jnp.where(first, a, pltpu.roll(b, half, 1))
-        power_ref[m, 0] = jnp.where(first, pltpu.roll(a, half, 1), b)
+    a, b = maps[0].astype(jnp.float32), maps[1].astype(jnp.float32)
+    peak_ref[0, 0] = jnp.where(first, a, pltpu.roll(b, half, 1))
+    power_ref[0, 0] = jnp.where(first, pltpu.roll(a, half, 1), b)
 
 
 def shards_fused(spectra, bank, orient_index):
@@ -564,8 +563,13 @@
         ),
     )(orient_index, spectra, bank, *tables)
     out = jax.ShapeDtypeStruct((2, 1, band, WCOLS), f32)
+    one_mic = pl.BlockSpec((1, 1, band, WCOLS), lambda m: (m, 0, 0, 0))
     return pl.pallas_call(
-        assemble_kernel, out_shape=(out, out), in_specs=[vmem], out_specs=(vmem, vmem)
+        assemble_kernel,
+        grid=(2,),
+        out_shape=(out, out),
+        in_specs=[pl.BlockSpec((2, band, WCOLS), lambda m: (m, 0, 0))],
+        out_specs=(one_mic, one_mic),
     )(maps)
 
 

time: 70.3 us -> 70.1 us (level)
  no operation moved by 1% of the time
where the time goes in v4:
time: 70.1 us; the launch traced here: 69.9 us
  Pallas kernels  69.3 us (99%)
    pallas_call x1, Pallas kernels, shards_fused(): pl.pallas_call(functools.partial(fused_kernel, (bands, share, band, lengt...  67.2 us
    pallas_call x1, Pallas kernels, shards_fused(): pl.pallas_call(assemble_kernel, grid=(2,), out_shape=(out, out), in_specs...  2.03 us

profile of v4, /device:TPU:0, one launch (start us, length us, event | category | flops | bytes accessed | tf_op | source)
XLA Modules:
  0.0 69.9 jit_solution(17775715915057831368)
XLA Ops:
  0.6 67.2 %shard_map.86.maps = bf16[4,512,128]{2,1,0:T(8,128)(2,1)} custom-call(s32[8]{0:T(128)} %index_ref.1, bf16[2,2,512,2048]{3,2,1,0:T(8,128)(2,1)} %spectra_ref.1, bf16[8,384,384]{2,1,0:T(8,128)(2,1)} %bank_ref.1, f32[2,192,384]{2,1,0:T(8,128)} %constant.8.clone.w384, f32[2,80,512]{2,1,0:T(8,128)} %constant.9.clone.w512, f32[2,160,256]{2,1,0:T(8,128)} %constant.10.clone.w256, ...), custom_call_target="tpu_custom_call" | custom-call | tf_op jit(solution)/shard_map/pallas_call | solution.py:520
  67.9 2.0 %shard_map.87 = (f32[2,1,512,128]{3,2,1,0:T(8,128)}, f32[2,1,512,128]{3,2,1,0:T(8,128)}) custom-call(bf16[4,512,128]{2,1,0:T(8,128)(2,1)} %shard_map.86.maps), custom_call_target="tpu_custom_call" | custom-call | tf_op jit(solution)/shard_map/pallas_call | solution.py:567
